TPU v7x, 32 devices: a whole 2x2x4 slice. The times are simulated.
32 devices in a mesh: dp: 2 (over core), order: 8 (over z, y), ens: 2 (over x).
Axes of the slice: x: 2, y: 2, z: 4, core: 2. Of those that a mesh axis runs over, the one named last changes fastest.
Arguments:
- fourier: bfloat16 [2, 16, 320, 40960], P('dp', 'ens', 'order'), may hold values from -20 to 20
- analysis: bfloat16 [320, 320, 320], P(None, 'order'), may hold values from -0.3125 to 0.3125
- target: bfloat16 [2, 320, 40960], P('dp', 'ens', 'order'), may hold values from -6 to 6
- band_ids: int32 [320, 320], P('ens', 'order'), may hold values from 0 to 15, as said below
- partners: int32 [16, 4], replicated, may hold values from 0 to 15, as said below
- band_cotangent: float32 [2, 16], replicated, may hold values from 0.5 to 4
Outputs:
- grad_fourier: bfloat16 [2, 16, 320, 40960], P('dp', 'ens', 'order')
- grad_analysis: float32 [320, 320, 320], P(('dp', 'ens'), 'order')
- loss_bands: float32 [16], replicated
Inputs may be any that keep to these rules, and one draw needn't show every extreme that they name: band_ids[l,m] depends on l only, never falls as l grows, starts at 0 and takes every band from 0 to 15. `partners`: each row names 4 different members, none equal to the row's own member.
All inputs are finite; a program needn't handle non-finite values.
Results may differ from a plain program's by a relative error of at most 0.0085.
Values may be sent and summed in bfloat16 or wider, within the bound.
A program may use at most 256 MiB of HBM per device.

v0:
```python
import jax
import jax.numpy as jnp
from jax import lax
from jax.sharding import PartitionSpec as P

MEMBERS = 16
NLAT = 320
L = 320
C = 64
NBANDS = 16
PARTNERS = 4


HIGHEST = lax.Precision.HIGHEST
EPSILON = 1e-06
WEIGHT_RATIO = 1.0 / 64.0


def band_terms(grams, partners, cotangent):
    diagonal_part = jnp.diagonal(grams, axis1=2, axis2=3)
    squared = diagonal_part[..., :, None] + diagonal_part[..., None, :] - 2.0 * grams
    distance = jnp.sqrt(squared + EPSILON)
    member_ids = jnp.arange(MEMBERS, dtype=jnp.int32)
    counts = jnp.sum(
        (partners[:, :, None] == member_ids[None, None, :]).astype(jnp.float32), axis=1
    )
    obs_dist = distance[:, :, :MEMBERS, MEMBERS]
    pair_dist = distance[:, :, :MEMBERS, :MEMBERS]
    scores = jnp.mean(obs_dist, axis=-1) - jnp.sum(counts * pair_dist, axis=(-2, -1)) / (
        2.0 * MEMBERS * PARTNERS
    )
    scaled = cotangent * (16.0 * MEMBERS * NLAT)
    symmetric = counts + counts.T
    obs_weight = scaled[..., None] / (MEMBERS * obs_dist)
    pair_weight = scaled[..., None, None] * symmetric / (2.0 * MEMBERS * PARTNERS * pair_dist)
    identity = jnp.eye(MEMBERS, dtype=jnp.float32)
    member_part = pair_weight + identity * (obs_weight - jnp.sum(pair_weight, axis=-1))[..., None]
    mixing = jnp.concatenate([member_part, -obs_weight[..., None]], axis=-1)
    return (scores, mixing)


def body(fourier, analysis, target, band_ids, partners, band_cotangent):
    samples = fourier.shape[0]
    own_members = fourier.shape[1]
    orders = analysis.shape[1]
    width = 2 * C
    degrees_here = band_ids.shape[0]
    order_start = lax.axis_index("order") * orders
    degree_start = lax.axis_index("ens") * degrees_here
    order_index = order_start + jnp.arange(orders, dtype=jnp.int32)
    all_degrees = jnp.arange(L, dtype=jnp.int32)
    keep_all = all_degrees[:, None] >= order_index[None, :]
    local_degrees = degree_start + jnp.arange(degrees_here, dtype=jnp.int32)
    keep_here = local_degrees[:, None] >= order_index[None, :]
    rows = lax.all_to_all(fourier, "order", split_axis=3, concat_axis=2, tiled=True)
    items = rows.shape[1]
    grid = rows.reshape(samples, items, NLAT, orders, width)
    spec = jnp.einsum("bitmq,tml->bilmq", grid, analysis, preferred_element_type=jnp.float32)
    spec = jnp.where(keep_all[None, None, :, :, None], spec, 0.0).astype(jnp.bfloat16)
    grid_rows = rows
    spectra = spec.reshape(samples, items, L, orders * width)
    gathered = lax.all_to_all(spectra, "ens", split_axis=2, concat_axis=1, tiled=True)
    predicted = gathered.reshape(samples, MEMBERS, degrees_here, orders, width)
    observed = target.reshape(samples, degrees_here, orders, width)
    observed = jnp.where(keep_here[None, :, :, None], observed, jnp.zeros((), jnp.bfloat16))
    stacked = jnp.concatenate([predicted, observed[:, None]], axis=1)
    pair_terms = jnp.einsum(
        "bilmq,bjlmq->bijlm", stacked, stacked, preferred_element_type=jnp.float32
    )
    band_range = jnp.arange(NBANDS, dtype=jnp.int32)
    one_hot = (band_ids[:, :, None] == band_range[None, None, :]).astype(jnp.float32)
    grams = jnp.einsum("bijlm,lmk->bkij", pair_terms, one_hot, precision=HIGHEST)
    sample_start = lax.axis_index("dp") * samples
    grams = lax.psum(grams, ("order", "ens"))
    cotangent = lax.dynamic_slice_in_dim(band_cotangent, sample_start, samples, 0)
    scores, mixing = band_terms(grams, partners, cotangent)
    loss_bands = lax.psum(jnp.sum(cotangent * scores, axis=0), "dp")
    spread = jnp.einsum("lmk,bkij->blmij", one_hot, mixing, precision=HIGHEST)
    grad_spec = jnp.einsum(
        "blmij,bjlmq->bilmq", spread, stacked.astype(jnp.float32), precision=HIGHEST
    ).astype(jnp.bfloat16)
    grad_spec = grad_spec.reshape(samples, MEMBERS, degrees_here, orders * width)
    returned = lax.all_to_all(grad_spec, "ens", split_axis=1, concat_axis=2, tiled=True)
    back = returned.reshape(samples, own_members, L, orders, width)
    grid_own = grid_rows.reshape(samples, own_members, NLAT, orders, width)
    rows = grid_own
    halves = lax.psum_scatter(
        (
            jnp.einsum("bitmq,bilmq->tml", rows, back, preferred_element_type=jnp.float32)
            * WEIGHT_RATIO
        ).astype(jnp.bfloat16),
        "dp",
        scatter_dimension=0,
        tiled=True,
    )
    grad_analysis = lax.psum_scatter(halves, "ens", scatter_dimension=0, tiled=True).astype(
        jnp.float32
    )
    grid_grad = jnp.einsum(
        "bilmq,tml->bitmq", back, analysis, preferred_element_type=jnp.float32
    ).astype(jnp.bfloat16)
    grid_grad = grid_grad.reshape(samples, own_members, NLAT, orders * width)
    grad_fourier = lax.all_to_all(grid_grad, "order", split_axis=2, concat_axis=3, tiled=True)
    return (grad_fourier, grad_analysis, loss_bands)


def joint_body(fourier, analysis, target, band_ids, partners, band_cotangent):
    samples, own_members, own_rows, columns = fourier.shape
    rows_parts = lax.axis_size("order")
    ens_parts = lax.axis_size("ens")
    parts = rows_parts * ens_parts
    width = 2 * C
    orders = analysis.shape[1]
    own_orders = orders // ens_parts
    members = own_members * ens_parts
    ens_index = lax.axis_index("ens")
    order_start = lax.axis_index("order") * orders + ens_index * own_orders
    order_index = order_start + jnp.arange(own_orders, dtype=jnp.int32)
    keep = jnp.arange(L, dtype=jnp.int32)[None, :] >= order_index[:, None]

    weights = lax.dynamic_slice_in_dim(analysis, ens_index * own_orders, own_orders, 1)
    weights = jnp.transpose(weights, (1, 0, 2))

    sent = fourier.reshape(samples * own_members, own_rows, parts, own_orders * width)
    sent = jnp.transpose(sent, (2, 0, 1, 3))
    got = lax.all_to_all(sent, ("order", "ens"), split_axis=0, concat_axis=0, tiled=True)
    got = got.reshape(rows_parts, ens_parts, samples, own_members, own_rows, own_orders, width)
    grid = jnp.transpose(got, (2, 5, 0, 4, 1, 3, 6))
    grid = grid.reshape(samples, own_orders, NLAT, members * width)

    spec = jnp.einsum("bmtx,mtl->bmlx", grid, weights, preferred_element_type=jnp.float32)
    spec = jnp.where(keep[None, :, :, None], spec, 0.0).astype(jnp.bfloat16)
    spec = spec.reshape(samples, own_orders, L, members, width)

    observed = lax.all_to_all(target, "ens", split_axis=2, concat_axis=1, tiled=True)
    observed = observed.reshape(samples, L, own_orders, width)
    observed = jnp.transpose(observed, (0, 2, 1, 3))
    observed = jnp.where(keep[None, :, :, None], observed, jnp.zeros((), jnp.bfloat16))

    stacked = jnp.concatenate([spec, observed[:, :, :, None]], axis=3)
    pair_terms = jnp.einsum(
        "bmliq,bmljq->blij", stacked, stacked, preferred_element_type=jnp.float32
    )
    bands = lax.all_gather(band_ids[:, 0], "ens", axis=0, tiled=True)
    band_range = jnp.arange(NBANDS, dtype=jnp.int32)
    one_hot = (bands[:, None] == band_range[None, :]).astype(jnp.float32)
    grams = jnp.einsum("blij,lk->bkij", pair_terms, one_hot, precision=HIGHEST)
    grams = lax.psum(grams, ("order", "ens"))
    sample_start = lax.axis_index("dp") * samples
    cotangent = lax.dynamic_slice_in_dim(band_cotangent, sample_start, samples, 0)
    scores, mixing = band_terms(grams, partners, cotangent)
    loss_bands = lax.psum(jnp.sum(cotangent * scores, axis=0), "dp")

    spread = jnp.einsum("lk,bkij->blij", one_hot, mixing, precision=HIGHEST)
    high = lax.reduce_precision(spread, 8, 7)
    split = jnp.concatenate([high, spread - high], axis=2).astype(jnp.bfloat16)
    both = jnp.einsum(
        "blij,bmljq->bmliq", split, stacked, preferred_element_type=jnp.float32
    )
    grad_spec = (both[:, :, :, :members] + both[:, :, :, members:]).astype(jnp.bfloat16)
    grad_spec = grad_spec.reshape(samples, own_orders, L, members * width)

    grid_grad = jnp.einsum(
        "bmlx,mtl->bmtx", grad_spec, weights, preferred_element_type=jnp.float32
    ).astype(jnp.bfloat16)
    grid_grad = grid_grad.reshape(
        samples, own_orders, rows_parts, own_rows, ens_parts, own_members, width
    )
    home = jnp.transpose(grid_grad, (2, 4, 0, 5, 3, 1, 6))
    home = home.reshape(parts, samples * own_members, own_rows, own_orders * width)
    home = lax.all_to_all(home, ("order", "ens"), split_axis=0, concat_axis=0, tiled=True)
    grad_fourier = jnp.transpose(home, (1, 2, 0, 3)).reshape(
        samples, own_members, own_rows, columns
    )

    weight_grad = (
        jnp.einsum("bmtx,bmlx->tml", grid, grad_spec, preferred_element_type=jnp.float32)
        * WEIGHT_RATIO
    ).astype(jnp.bfloat16)
    halves = lax.psum_scatter(weight_grad, "dp", scatter_dimension=0, tiled=True)
    grad_analysis = lax.all_to_all(
        halves, "ens", split_axis=0, concat_axis=1, tiled=True
    ).astype(jnp.float32)
    return (grad_fourier, grad_analysis, loss_bands)


def solution(mesh):
    placed = (
        P("dp", "ens", "order", None),
        P(None, "order", None),
        P("dp", "ens", "order"),
        P("ens", "order"),
        P(),
        P(),
    )
    groups = mesh.shape["order"] * mesh.shape["ens"]
    divides = (L % groups) == 0
    return jax.shard_map(
        joint_body if divides else body,
        mesh=mesh,
        in_specs=placed,
        out_specs=(P("dp", "ens", "order", None), P(("dp", "ens"), "order", None), P()),
        check_vma=False,
    )
```

profile of v0, /device:TPU:14, one launch (start us, length us, event | category | flops | bytes accessed | tf_op | source)
XLA Modules:
  0.0 1918.2 jit_solution(2085818638308268628)
XLA Ops:
  18.8 29.1 %reduce.4 = bf16[5120,160]{1,0:T(8,128)(2,1)S(1)} reduce(bf16[5120,1,160]{2,1,0:T(2,128)(2,1)} %bitcast.132, bf16[]{:T(256)} %broadcast.160), dimensions={1}, to_apply=%bitcast.105.reduce_sub_computation | reduce | bytes 3276802
  57.0 18.9 copy.192
  75.9 18.5 copy.214
  122.8 84.3 %all-reduce = s32[320]{0:T(512)S(1)} all-reduce(s32[320]{0:T(512)S(1)} %dynamic-update-slice), channel_id=2, replica_groups=mesh['dp'=2,'order'=8,'ens'=2] {'ens'}, use_global_device_ids=true, to_apply=%add | all-reduce | flops 320 | bytes 2560
  234.9 449.5 %all-to-all-done = bf16[16,8,40,2560]{3,2,1,0:T(8,128)(2,1)} async-done(((bf16[16,8,40,2560]{3,2,1,0:T(8,128)(2,1)}), bf16[16,8,40,2560]{3,2,1,0:T(8,128)(2,1)}, u32[]{:S(2)}, u32[]{:S(2)}) %all-to-all-start) | async-done | bytes 26214432 | tf_op jit(solution)/shard_map/all_to_all | solution.py:126
  684.4 44.0 %reshape.215 = bf16[8,2,1,8,40,20,128]{6,5,4,3,1,0,2:T(8,128)(2,1)} reshape(bf16[16,8,40,2560]{3,2,1,0:T(8,128)(2,1)} %all-to-all-done) | data formatting | bytes 52428800 | tf_op jit(solution)/shard_map/reshape | solution.py:127
  728.4 19.8 %copy.152 = bf16[1,20,8,40,2,8,128]{6,5,4,3,2,1,0:T(8,128)(2,1)} copy(bf16[1,20,8,40,2,8,128]{6,1,3,5,4,2,0:T(8,128)(2,1)} %bitcast.122) | data formatting | bytes 52428800 | tf_op jit(solution)/shard_map/transpose | solution.py:128
  748.2 38.7 %reshape.216 = bf16[20,320,2048]{2,1,0:T(8,128)(2,1)} reshape(bf16[1,20,8,40,2,8,128]{6,5,4,3,2,1,0:T(8,128)(2,1)} %copy.152) | data formatting | bytes 52428800 | tf_op jit(solution)/shard_map/reshape.1
  786.9 28.7 %select_convert_fusion = bf16[20,320,2048]{2,1,0:T(8,128)(2,1)} fusion(bf16[20,320,2048]{2,1,0:T(8,128)(2,1)} %reshape.216, pred[20,320]{1,0:T(8,128)(4,1)S(1)} %iota_compare_fusion, bf16[320,20,320]{0,2,1:T(8,128)(2,1)} %copy.191), kind=kOutput, calls=%fused_computation.3 | convolution fusion | flops 8414822400 | bytes 56531200 | tf_op jit(solution)/shard_map/bmtx,mtl->bmlx/dot_general | solution.py:131
  815.6 18.1 copy.193
  833.8 23.4 %fusion.14 = f32[320,17,17]{2,1,0:T(8,128)} fusion(bf16[1,20,320,1,128]{4,3,1,2,0:T(2,128)(2,1)S(1)} %copy.159, bf16[1,20,320,16,128]{4,3,2,1,0:T(8,128)(2,1)} %bitcast.124), kind=kOutput, calls=%fused_computation.19 | convolution fusion | flops 529203200 | bytes 28222720 | tf_op jit(solution)/shard_map/bmliq,bmljq->blij/dot_general | solution.py:141
  864.3 80.1 %psum.14 = f32[1,16,17,17]{2,1,3,0:T(8,128)S(1)} all-reduce(f32[1,16,17,17]{2,1,3,0:T(8,128)S(1)} %convolution_bitcast_fusion.2), channel_id=1, replica_groups=mesh['dp'=2,'order'=8,'ens'=2] {'order','ens'}, use_global_device_ids=true, to_apply=%region_1.2 | all-reduce | flops 4624 | bytes 36992 | tf_op jit(solution)/shard_map/psum | solution.py:148
  957.0 45.4 %convolution_bitcast_fusion = f32[1,20,320,32,128]{4,3,1,2,0:T(8,128)} fusion(bf16[320,32,17,1]{1,2,3,0:T(8,128)(2,1)} %copy.182, bf16[1,20,320,1,128]{4,3,1,2,0:T(2,128)(2,1)S(1)} %copy.159, bf16[1,20,320,16,128]{4,3,2,1,0:T(8,128)(2,1)} %bitcast.125), kind=kOutput, calls=%fused_computation.5 | convolution fusion | flops 946995200 | bytes 133058560 | tf_op jit(solution)/shard_map/blij,bmljq->bmliq/dot_general | solution.py:157
  1002.4 41.7 %fusion = bf16[1,20,320,16,128]{4,3,1,2,0:T(8,128)(2,1)} fusion(f32[1,20,320,32,128]{4,3,1,2,0:T(8,128)} %convolution_bitcast_fusion), kind=kLoop, calls=%fused_computation.2 | loop fusion | flops 26214400 | bytes 131072000 | tf_op jit(solution)/shard_map/convert_element_type | solution.py:160
  1044.2 43.6 %reshape.246 = bf16[20,320,2048]{2,0,1:T(8,128)(2,1)} reshape(bf16[1,20,320,16,128]{4,3,1,2,0:T(8,128)(2,1)} %fusion) | data formatting | bytes 52428800 | tf_op jit(solution)/shard_map/reshape.36
  1087.7 29.2 %fusion.9 = bf16[320,20,320]{0,2,1:T(8,128)(2,1)} fusion(bf16[20,320,2048]{2,1,0:T(8,128)(2,1)} %reshape.216, bf16[20,320,2048]{2,0,1:T(8,128)(2,1)} %reshape.246), kind=kOutput, calls=%fused_computation.15 | convolution fusion | flops 8392704000 | bytes 56524800 | tf_op jit(solution)/shard_map/bmtx,bmlx->tml/dot_general | solution.py:177
  1126.2 23.2 %reduce-scatter.2.cloned.1.call-done = bf16[160,20,320]{2,1,0:T(8,128)(2,1)} async-done(((bf16[320,20,320]{2,1,0:T(8,128)(2,1)}), bf16[160,20,320]{2,1,0:T(8,128)(2,1)}) %reduce-scatter.2.cloned.1.call-update) | async-done | bytes 2048016 | tf_op jit(solution)/shard_map/reduce_scatter | solution.py:180
  1154.5 27.5 %fusion.6 = bf16[20,320,2048]{2,1,0:T(8,128)(2,1)} fusion(bf16[20,320,2048]{2,0,1:T(8,128)(2,1)} %reshape.246, bf16[320,20,320]{0,2,1:T(8,128)(2,1)} %copy.191), kind=kOutput, calls=%fused_computation.13 | convolution fusion | flops 8401715200 | bytes 56524800 | tf_op jit(solution)/shard_map/bmlx,mtl->bmtx/dot_general | solution.py:163
  1182.1 18.1 copy.194
  1200.2 25.0 %copy.213 = bf16[1,20,8,40,2,8,128]{6,1,3,5,4,2,0:T(8,128)(2,1)} copy(bf16[1,20,8,40,2,8,128]{6,5,4,3,2,1,0:T(8,128)(2,1)} %bitcast.126) | data formatting | bytes 52428800 | tf_op jit(solution)/shard_map/reshape | solution.py:166
  1225.1 43.8 %reshape.223 = bf16[16,8,40,2560]{3,2,1,0:T(8,128)(2,1)} reshape(bf16[8,2,1,8,40,20,128]{6,5,4,3,1,0,2:T(8,128)(2,1)} %bitcast.123) | data formatting | bytes 52428800 | tf_op jit(solution)/shard_map/reshape | solution.py:170
  1283.4 574.2 %all-to-all-done.2 = bf16[16,8,40,2560]{3,2,1,0:T(8,128)(2,1)} async-done(((bf16[16,8,40,2560]{3,2,1,0:T(8,128)(2,1)}), bf16[16,8,40,2560]{3,2,1,0:T(8,128)(2,1)}, u32[]{:S(2)}, u32[]{:S(2)}) %all-to-all-start.2) | async-done | bytes 26214432 | tf_op jit(solution)/shard_map/all_to_all | solution.py:171
  1857.6 18.5 copy.173
  1876.2 34.9 %reshape.224 = bf16[1,8,40,40960]{3,2,1,0:T(8,128)(2,1)} reshape(bf16[8,40,16,2560]{3,2,1,0:T(8,128)(2,1)} %copy.173) | data formatting | bytes 52428800 | tf_op jit(solution)/shard_map/reshape | solution.py:172
  (72 shorter events, 124.7 us)
Async XLA Ops:
  52.8 41.6 %all-to-all-start.1 = ((bf16[2,2,204800]{2,1,0:T(2,128)(2,1)}), bf16[2,2,204800]{2,1,0:T(2,128)(2,1)S(1)}, u32[]{:S(2)}, u32[]{:S(2)}) async-start(bf16[2,2,204800]{2,1,0:T(2,128)(2,1)} %reshape.247), calls=%async_computation.1 | async-start | bytes 3276800 | tf_op jit(solution)/shard_map/all_to_all | solution.py:135
  94.4 7.9 copy-start.4
  94.4 27.0 %copy-start.7 = (u32[32]{0:T(128)S(1)}, u32[32]{0:T(128)}, u32[]{:S(2)}) copy-start(u32[32]{0:T(128)} %constant.64) | copy-start | bytes 388
  94.4 28.2 %slice-start = ((s32[160,40]{0,1:T(8,128)}), s32[160,1]{0,1:T(1,128)S(1)}, s32[]{:S(2)}) async-start(s32[160,40]{0,1:T(8,128)} %param.9), calls=%async_computation.6 | async-start | bytes 2048 | tf_op jit(solution)/shard_map/slice | solution.py:144
  94.4 113.3 %copy-start.5 = (f32[2,16]{1,0:T(2,128)S(1)}, f32[2,16]{1,0:T(2,128)}, u32[]{:S(2)}) copy-start(f32[2,16]{1,0:T(2,128)} %param.11) | copy-start | bytes 388
  94.4 590.0 %all-to-all-start = ((bf16[16,8,40,2560]{3,2,1,0:T(8,128)(2,1)}), bf16[16,8,40,2560]{3,2,1,0:T(8,128)(2,1)}, u32[]{:S(2)}, u32[]{:S(2)}) async-start(bf16[16,8,40,2560]{3,2,1,0:T(8,128)(2,1)} %bitcast.127), calls=%async_computation | async-start | bytes 52428800 | tf_op jit(solution)/shard_map/all_to_all | solution.py:126
  101.7 1047.7 %reduce-scatter.2.cloned.1.call-start = ((), (), s32[]{:S(2)}) async-start(), calls=%async_computation.5 | async-start | bytes 8847360 | tf_op jit(solution)/shard_map/reduce_scatter | solution.py:180
  102.4 112.3 %copy-start = (f32[16,16]{0,1:T(8,128)}, f32[16,16]{0,1:T(8,128)S(1)}, u32[]{:S(2)}) copy-start(f32[16,16]{0,1:T(8,128)S(1)} %copy.160) | copy-start | bytes 3076
  207.2 655.0 %copy-start.1 = (s32[320]{0:T(512)}, s32[320]{0:T(512)S(1)}, u32[]{:S(2)}) copy-start(s32[320]{0:T(512)S(1)} %all-reduce) | copy-start | bytes 3844
  1149.4 119.5 %all-to-all-start.3 = ((bf16[160,20,320]{2,1,0:T(8,128)(2,1)}), bf16[160,20,320]{2,1,0:T(8,128)(2,1)S(1)}, u32[]{:S(2)}, u32[]{:S(2)}) async-start(bf16[160,20,320]{2,1,0:T(8,128)(2,1)} %reduce-scatter.2.cloned.1.call-done), calls=%async_computation.4 | async-start | bytes 5898240 | tf_op jit(solution)/shard_map/all_to_all | solution.py:181
  1268.9 6.5 copy-start.2
  1268.9 6.5 copy-start.3
  1269.0 6.5 copy-start.6
  1269.0 588.7 %all-to-all-start.2 = ((bf16[16,8,40,2560]{3,2,1,0:T(8,128)(2,1)}), bf16[16,8,40,2560]{3,2,1,0:T(8,128)(2,1)}, u32[]{:S(2)}, u32[]{:S(2)}) async-start(bf16[16,8,40,2560]{3,2,1,0:T(8,128)(2,1)} %reshape.223), calls=%async_computation.2 | async-start | bytes 52428800 | tf_op jit(solution)/shard_map/all_to_all | solution.py:171
Sparse Core Ops, SparseCore 0:
  1126.3 23.0 reduce-scatter.1
where the time goes:
time: 1950 us; the launch traced here: 1920 us
  waiting for transfers between devices  1050 us (54%)
  local copies, waits for them, and re-layouts  428 us (22%)
  blocking collectives  167 us (9%)
  matrix products  158 us (8%)
  other arithmetic  79.3 us (4%)
  starting transfers between devices  23.6 us (1%)
    all_to_all x1, waiting for transfers between devices, joint_body(): lax.all_to_all(home, ('order', 'ens'), split_axis=0, concat_axis=0, tiled...  574 us
    all_to_all x1, waiting for transfers between devices, joint_body(): lax.all_to_all(sent, ('order', 'ens'), split_axis=0, concat_axis=0, tiled...  449 us
    unnamed x28, local copies, waits for them, and re-layouts  91.2 us
    unnamed x1, blocking collectives  84.3 us
    another operation x3, local copies, waits for them, and re-layouts  82.5 us
    psum x1, blocking collectives, joint_body(): grams = lax.psum(grams, ('order', 'ens'))  80.1 us
    dot_general x1, matrix products, joint_body(): jnp.einsum('blij,bmljq->bmliq', split, stacked, preferred_element_type=jn...  45.4 us
    reshape x1, local copies, waits for them, and re-layouts, joint_body(): got.reshape(rows_parts, ens_parts, samples, own_members, own_rows, own_or...  44 us
  transfers between devices with their start and end apart: 5, of which 3 were waited for; matrix products, arithmetic and copies ran while one was open for 11% of the time, Pallas kernels for 0%

commit v1 on v0

--- a/solution.py
+++ b/solution.py
@@ -1,6 +1,10 @@
+import functools
+
 import jax
 import jax.numpy as jnp
 from jax import lax
+from jax.experimental import pallas as pl
+from jax.experimental.pallas import tpu as pltpu
 from jax.sharding import PartitionSpec as P
 
 MEMBERS = 16
@@ -104,84 +108,483 @@
     return (grad_fourier, grad_analysis, loss_bands)
 
 
-def joint_body(fourier, analysis, target, band_ids, partners, band_cotangent):
-    samples, own_members, own_rows, columns = fourier.shape
-    rows_parts = lax.axis_size("order")
-    ens_parts = lax.axis_size("ens")
-    parts = rows_parts * ens_parts
-    width = 2 * C
-    orders = analysis.shape[1]
-    own_orders = orders // ens_parts
-    members = own_members * ens_parts
-    ens_index = lax.axis_index("ens")
-    order_start = lax.axis_index("order") * orders + ens_index * own_orders
-    order_index = order_start + jnp.arange(own_orders, dtype=jnp.int32)
-    keep = jnp.arange(L, dtype=jnp.int32)[None, :] >= order_index[:, None]
-
-    weights = lax.dynamic_slice_in_dim(analysis, ens_index * own_orders, own_orders, 1)
+MESH = pl.DeviceIdType.MESH
+LANES = 128
+BLOCK = 16
+ROWS = MEMBERS * BLOCK
+PAIR = 2
+VMEM_LIMIT = 64000 * 1024
+
+
+def my_place():
+    return lax.axis_index("dp"), lax.axis_index("order"), lax.axis_index("ens")
+
+
+def other_places(orders, enses):
+    core, order, ens = my_place()
+    places = []
+    for step in range(1, orders * enses):
+        flat = lax.rem(order * enses + ens + step, orders * enses)
+        places.append((core, flat // enses, lax.rem(flat, enses)))
+    return places
+
+
+def greet(places):
+    barrier = pltpu.get_barrier_semaphore()
+    for place in places:
+        pl.semaphore_signal(barrier, inc=1, device_id=place, device_id_type=MESH)
+    pl.semaphore_wait(barrier, len(places))
+
+
+def gather_kernel(
+    orders, enses, fourier, target, onehot, grid, observed, bands, held, held_obs, held_hot,
+    send, recv, send_obs, recv_obs, own_sem
+):
+    core, order, ens = my_place()
+    members, rows = fourier.shape[0], fourier.shape[1]
+    width = grid.shape[2]
+    degrees = target.shape[0]
+    places = other_places(orders, enses)
+    greet(places)
+    copies = []
+
+    def columns(flat):
+        return pl.ds(pl.multiple_of(flat * width, LANES), width)
+
+    grid_to = grid.at[pl.ds(ens * members, members), pl.ds(order * rows, rows)]
+    obs_to = observed.at[pl.ds(ens * degrees, degrees)]
+    hot_to = bands.at[pl.ds(ens * degrees, degrees)]
+    for step in range(1, enses):
+        other = lax.rem(ens + step, enses)
+        place = (core, order, other)
+        for k, (source, goal) in enumerate(
+            ((target.at[:, columns(other)], obs_to), (onehot, hot_to))
+        ):
+            copies.append(
+                pltpu.make_async_remote_copy(
+                    source, goal, send_obs.at[step, k], recv_obs.at[step, k],
+                    device_id=place, device_id_type=MESH,
+                )
+            )
+            copies[-1].start()
+    for step, place in enumerate(places):
+        copies.append(
+            pltpu.make_async_remote_copy(
+                fourier.at[:, :, columns(place[1] * enses + place[2])], grid_to,
+                send.at[step], recv.at[step], device_id=place, device_id_type=MESH,
+            )
+        )
+        copies[-1].start()
+    own = (
+        (fourier.at[:, :, columns(order * enses + ens)], held, grid_to),
+        (target.at[:, columns(ens)], held_obs, obs_to),
+        (onehot, held_hot, hot_to),
+    )
+    first = [pltpu.make_async_copy(a, b, own_sem.at[0, k]) for k, (a, b, _) in enumerate(own)]
+    second = [pltpu.make_async_copy(b, c, own_sem.at[1, k]) for k, (_, b, c) in enumerate(own)]
+    for copy in first:
+        copy.start()
+    for one, two in zip(first, second):
+        one.wait()
+        two.start()
+    for copy in second:
+        copy.wait()
+    for copy in copies:
+        copy.wait()
+
+
+def gather_rows(orders, enses, fourier, target, onehot):
+    members, rows, columns = fourier.shape
+    width = columns // (orders * enses)
+    degrees = target.shape[0]
+    peers = orders * enses - 1
+    anywhere = pl.BlockSpec(memory_space=pl.ANY)
+    return pl.pallas_call(
+        functools.partial(gather_kernel, orders, enses),
+        out_shape=(
+            jax.ShapeDtypeStruct((members * enses, rows * orders, width), fourier.dtype),
+            jax.ShapeDtypeStruct((degrees * enses, width), target.dtype),
+            jax.ShapeDtypeStruct((degrees * enses, LANES), onehot.dtype),
+        ),
+        in_specs=[anywhere] * 3,
+        out_specs=(anywhere,) * 3,
+        scratch_shapes=[
+            pltpu.VMEM((members, rows, width), fourier.dtype),
+            pltpu.VMEM((degrees, width), target.dtype),
+            pltpu.VMEM((degrees, LANES), onehot.dtype),
+            pltpu.SemaphoreType.DMA((peers,)),
+            pltpu.SemaphoreType.DMA((peers,)),
+            pltpu.SemaphoreType.DMA((enses, 2)),
+            pltpu.SemaphoreType.DMA((enses, 2)),
+            pltpu.SemaphoreType.DMA((2, 3)),
+        ],
+        compiler_params=pltpu.CompilerParams(
+            collective_id=0, has_side_effects=True, vmem_limit_bytes=VMEM_LIMIT
+        ),
+        name="gather_rows",
+    )(fourier, target, onehot)
+
+
+def scatter_kernel(
+    orders, enses, gradient, weight_grad, home, shares, held, held_share,
+    send, recv, send_share, recv_share, own_sem
+):
+    core, order, ens = my_place()
+    members, rows = home.shape[0], home.shape[1]
+    width = gradient.shape[2]
+    part = shares.shape[2]
+    places = other_places(orders, enses)
+    partners = [(1 - core, order, lax.rem(ens + step, enses)) for step in range(enses)]
+    greet(places + partners)
+    copies = []
+
+    def block(order_to, ens_to):
+        return gradient.at[pl.ds(ens_to * members, members), pl.ds(order_to * rows, rows)]
+
+    def share(core_to, ens_to):
+        return weight_grad.at[:, pl.ds((core_to * enses + ens_to) * part, part)]
+
+    home_to = home.at[
+        :, :, pl.ds(pl.multiple_of((order * enses + ens) * width, LANES), width)
+    ]
+    share_to = shares.at[core * enses + ens]
+    fellows = partners + [(core, order, lax.rem(ens + step, enses)) for step in range(1, enses)]
+    for step, place in enumerate(fellows):
+        copies.append(
+            pltpu.make_async_remote_copy(
+                share(place[0], place[2]), share_to, send_share.at[step], recv_share.at[step],
+                device_id=place, device_id_type=MESH,
+            )
+        )
+        copies[-1].start()
+    for step, place in enumerate(places):
+        copies.append(
+            pltpu.make_async_remote_copy(
+                block(place[1], place[2]), home_to, send.at[step], recv.at[step],
+                device_id=place, device_id_type=MESH,
+            )
+        )
+        copies[-1].start()
+    own = ((block(order, ens), held, home_to), (share(core, ens), held_share, share_to))
+    first = [pltpu.make_async_copy(a, b, own_sem.at[0, k]) for k, (a, b, _) in enumerate(own)]
+    second = [pltpu.make_async_copy(b, c, own_sem.at[1, k]) for k, (_, b, c) in enumerate(own)]
+    for copy in first:
+        copy.start()
+    for one, two in zip(first, second):
+        one.wait()
+        two.start()
+    for copy in second:
+        copy.wait()
+    for copy in copies:
+        copy.wait()
+
+
+def scatter_rows(orders, enses, cores, gradient, weight_grad):
+    members, rows, width = gradient.shape
+    members, rows = members // enses, rows // orders
+    own_orders, rows_all, degrees = weight_grad.shape
+    part = rows_all // (cores * enses)
+    peers = orders * enses - 1
+    fellows = cores * enses - 1
+    anywhere = pl.BlockSpec(memory_space=pl.ANY)
+    return pl.pallas_call(
+        functools.partial(scatter_kernel, orders, enses),
+        out_shape=(
+            jax.ShapeDtypeStruct((members, rows, width * orders * enses), gradient.dtype),
+            jax.ShapeDtypeStruct((cores * enses, own_orders, part, degrees), weight_grad.dtype),
+        ),
+        in_specs=[anywhere] * 2,
+        out_specs=(anywhere,) * 2,
+        scratch_shapes=[
+            pltpu.VMEM((members, rows, width), gradient.dtype),
+            pltpu.VMEM((own_orders, part, degrees), weight_grad.dtype),
+            pltpu.SemaphoreType.DMA((peers,)),
+            pltpu.SemaphoreType.DMA((peers,)),
+            pltpu.SemaphoreType.DMA((fellows,)),
+            pltpu.SemaphoreType.DMA((fellows,)),
+            pltpu.SemaphoreType.DMA((2, 2)),
+        ],
+        compiler_params=pltpu.CompilerParams(
+            collective_id=1, has_side_effects=True, vmem_limit_bytes=VMEM_LIMIT
+        ),
+        name="scatter_rows",
+    )(gradient, weight_grad)
+
+
+def contract(a, b, dims, precision=None):
+    return lax.dot_general(
+        a, b, (dims, ((), ())), precision=precision, preferred_element_type=jnp.float32
+    )
+
+
+NN = ((1,), (0,))
+NT = ((1,), (1,))
+TN = ((0,), (0,))
+
+
+def marks(shape, rule):
+    row = lax.broadcasted_iota(jnp.int32, shape, 0)
+    column = lax.broadcasted_iota(jnp.int32, shape, 1)
+    return rule(row, column)
+
+
+def as_float(flags):
+    return jnp.where(flags, 1.0, 0.0).astype(jnp.float32)
+
+
+def same_degree():
+    return marks((ROWS, ROWS), lambda r, c: lax.rem(r, BLOCK) == lax.rem(c, BLOCK))
+
+
+def same_member():
+    return marks((ROWS, ROWS), lambda r, c: r // BLOCK == c // BLOCK)
+
+
+def spread_bands(hot, rows_are_degrees):
+    repeat_band = as_float(marks((ROWS, LANES), lambda r, c: lax.rem(r, BLOCK) == c))
+    repeat_degree = as_float(marks((ROWS, BLOCK), lambda r, c: lax.rem(r, BLOCK) == c))
+    if rows_are_degrees:
+        wide = contract(repeat_degree, hot, NN)
+        full = contract(wide, repeat_band, NT)
+    else:
+        wide = contract(repeat_band, hot, NT)
+        full = contract(wide, repeat_degree, NT)
+    return jnp.where(same_member(), full, 0.0)
+
+
+def stack_members(ref, start):
+    block = ref[:, pl.ds(start, BLOCK), :]
+    return block.reshape(ROWS, block.shape[2])
+
+
+def spectra_kernel(orders, enses, own_orders, grid, weights, observed, bands, spec, sums, pairs, cross):
+    step = pl.program_id(0)
+    order_start = (lax.axis_index("order") * enses + lax.axis_index("ens")) * own_orders
+    degrees = spec.shape[1]
+    blocks = degrees // BLOCK
+
+    @pl.when(step == 0)
+    def _():
+        pairs[...] = jnp.zeros_like(pairs)
+        cross[...] = jnp.zeros_like(cross)
+
+    for k in range(PAIR):
+        keep = (
+            lax.broadcasted_iota(jnp.int32, (degrees, 2 * LANES), 0)
+            >= order_start + step * PAIR + k
+        )
+        matrix = weights[k]
+        lanes = slice(k * LANES, (k + 1) * LANES)
+        for i in range(0, MEMBERS, 2):
+            values = jnp.concatenate([grid[i, :, lanes], grid[i + 1, :, lanes]], axis=1)
+            out = contract(matrix, values, TN)
+            out = jnp.where(keep, out, 0.0).astype(jnp.bfloat16)
+            spec[i, :, lanes] = out[:, :LANES]
+            spec[i + 1, :, lanes] = out[:, LANES:]
+
+    @pl.loop(0, blocks)
+    def _(block):
+        start = pl.multiple_of(block * BLOCK, BLOCK)
+        member_rows = stack_members(spec, start)
+        row = lax.broadcasted_iota(jnp.int32, (BLOCK, PAIR * LANES), 0) + start
+        column = lax.broadcasted_iota(jnp.int32, (BLOCK, PAIR * LANES), 1) // LANES
+        seen = observed[pl.ds(start, BLOCK), :]
+        seen = jnp.where(row >= order_start + step * PAIR + column, seen.astype(jnp.float32), 0.0)
+        seen = seen.astype(jnp.bfloat16)
+        pairs[block] += contract(member_rows, member_rows, NT)
+        cross[block, :, :ROWS] += contract(seen, member_rows, NT)
+        cross[block, :, ROWS:] += contract(seen, jnp.concatenate([seen] * 8, axis=0), NT)
+
+    @pl.when(step == pl.num_programs(0) - 1)
+    def _():
+        sums[...] = jnp.zeros_like(sums)
+        pick_member = as_float(marks((MEMBERS, ROWS), lambda r, c: r == c // BLOCK))
+        pick_degree = marks((BLOCK, ROWS), lambda r, c: r == lax.rem(c, BLOCK))
+        pick_own = marks((BLOCK, LANES), lambda r, c: r == c)
+
+        @pl.loop(0, blocks)
+        def _(block):
+            start = pl.multiple_of(block * BLOCK, BLOCK)
+            hot = bands[pl.ds(start, BLOCK), :]
+            banded = spread_bands(hot, False)
+            matched = jnp.where(same_degree(), pairs[block], 0.0)
+            per_degree = contract(pick_member, matched, NN, HIGHEST)
+            with_obs = jnp.sum(
+                jnp.where(pick_degree, cross[block, :, :ROWS], 0.0), axis=0, keepdims=True
+            )
+            own_obs = jnp.sum(
+                jnp.where(pick_own, cross[block, :, ROWS:], 0.0), axis=1, keepdims=True
+            )
+            sums[:MEMBERS, :] += contract(per_degree, banded, NT, HIGHEST)
+            sums[MEMBERS : MEMBERS + 8, :] += contract(
+                jnp.broadcast_to(with_obs, (8, ROWS)), banded, NT, HIGHEST
+            )
+            sums[MEMBERS + 8 :, :LANES] += jnp.broadcast_to(
+                jnp.sum(hot * own_obs, axis=0, keepdims=True), (8, LANES)
+            )
+
+
+def spectra_call(orders, enses, grid, weights, observed, bands):
+    members, rows, width = grid.shape
+    own_orders = width // LANES
+    degrees = observed.shape[0]
+    blocks = degrees // BLOCK
+    steps = own_orders // PAIR
+    return pl.pallas_call(
+        functools.partial(spectra_kernel, orders, enses, own_orders),
+        grid=(steps,),
+        out_shape=(
+            jax.ShapeDtypeStruct((members, degrees, width), grid.dtype),
+            jax.ShapeDtypeStruct((MEMBERS + 16, ROWS), jnp.float32),
+        ),
+        in_specs=[
+            pl.BlockSpec((members, rows, PAIR * LANES), lambda s: (0, 0, s)),
+            pl.BlockSpec((PAIR, rows, degrees), lambda s: (s, 0, 0)),
+            pl.BlockSpec((degrees, PAIR * LANES), lambda s: (0, s)),
+            pl.BlockSpec((degrees, LANES), lambda s: (0, 0)),
+        ],
+        out_specs=(
+            pl.BlockSpec((members, degrees, PAIR * LANES), lambda s: (0, 0, s)),
+            pl.BlockSpec((MEMBERS + 16, ROWS), lambda s: (0, 0)),
+        ),
+        scratch_shapes=[
+            pltpu.VMEM((blocks, ROWS, ROWS), jnp.float32),
+            pltpu.VMEM((blocks, BLOCK, ROWS + LANES), jnp.float32),
+        ],
+        compiler_params=pltpu.CompilerParams(vmem_limit_bytes=VMEM_LIMIT),
+        name="spectra",
+    )(grid, weights, observed, bands)
+
+
+def gradient_kernel(
+    enses, own_orders, grid, spec, weights, observed, bands, mixing, out, weight_grad,
+    high, low, coefficients, mixed
+):
+    step = pl.program_id(0)
+    order_start = (lax.axis_index("order") * enses + lax.axis_index("ens")) * own_orders
+    degrees = spec.shape[1]
+    blocks = degrees // BLOCK
+
+    @pl.when(step == 0)
+    def _():
+        place_member = as_float(marks((LANES, ROWS), lambda r, c: r == c // BLOCK))
+
+        @pl.loop(0, blocks)
+        def _(block):
+            start = pl.multiple_of(block * BLOCK, BLOCK)
+            hot = bands[pl.ds(start, BLOCK), :]
+            banded = spread_bands(hot, True)
+            own = contract(banded, mixing[...], NN, HIGHEST)
+            full = jnp.where(same_degree(), contract(own, place_member, NN, HIGHEST), 0.0)
+            top = full.astype(jnp.bfloat16)
+            high[block] = top
+            low[block] = (full - top.astype(jnp.float32)).astype(jnp.bfloat16)
+            coefficients[block] = jnp.broadcast_to(
+                own[:, MEMBERS : MEMBERS + 1], (ROWS, LANES)
+            )
+
+    @pl.loop(0, blocks)
+    def _(block):
+        start = pl.multiple_of(block * BLOCK, BLOCK)
+        member_rows = stack_members(spec, start)
+        row = lax.broadcasted_iota(jnp.int32, (BLOCK, PAIR * LANES), 0) + start
+        column = lax.broadcasted_iota(jnp.int32, (BLOCK, PAIR * LANES), 1) // LANES
+        seen = observed[pl.ds(start, BLOCK), :].astype(jnp.float32)
+        seen = jnp.where(row >= order_start + step * PAIR + column, seen, 0.0)
+        total = contract(high[block], member_rows, NN) + contract(low[block], member_rows, NN)
+        factor = coefficients[block].reshape(MEMBERS, BLOCK, LANES)
+        factor = jnp.concatenate([factor] * PAIR, axis=2)
+        total = total.reshape(MEMBERS, BLOCK, PAIR * LANES) + factor * seen[None]
+        mixed[:, pl.ds(start, BLOCK), :] = total.astype(jnp.bfloat16)
+
+    for k in range(PAIR):
+        matrix = weights[k]
+        lanes = slice(k * LANES, (k + 1) * LANES)
+        slope = jnp.zeros((matrix.shape[0], degrees), jnp.float32)
+        for i in range(0, MEMBERS, 2):
+            both = jnp.concatenate([mixed[i, :, lanes], mixed[i + 1, :, lanes]], axis=1)
+            values = jnp.concatenate([grid[i, :, lanes], grid[i + 1, :, lanes]], axis=1)
+            rows = contract(matrix, both, NN).astype(jnp.bfloat16)
+            out[i, :, lanes] = rows[:, :LANES]
+            out[i + 1, :, lanes] = rows[:, LANES:]
+            slope += contract(values, both, NT)
+        weight_grad[k] = (slope * WEIGHT_RATIO).astype(jnp.bfloat16)
+
+
+def gradient_call(enses, grid, spec, weights, observed, bands, mixing):
+    members, rows, width = grid.shape
+    own_orders = width // LANES
+    degrees = observed.shape[0]
+    blocks = degrees // BLOCK
+    steps = own_orders // PAIR
+    return pl.pallas_call(
+        functools.partial(gradient_kernel, enses, own_orders),
+        grid=(steps,),
+        out_shape=(
+            jax.ShapeDtypeStruct((members, rows, width), grid.dtype),
+            jax.ShapeDtypeStruct((own_orders, rows, degrees), grid.dtype),
+        ),
+        in_specs=[
+            pl.BlockSpec((members, rows, PAIR * LANES), lambda s: (0, 0, s)),
+            pl.BlockSpec((members, degrees, PAIR * LANES), lambda s: (0, 0, s)),
+            pl.BlockSpec((PAIR, rows, degrees), lambda s: (s, 0, 0)),
+            pl.BlockSpec((degrees, PAIR * LANES), lambda s: (0, s)),
+            pl.BlockSpec((degrees, LANES), lambda s: (0, 0)),
+            pl.BlockSpec((ROWS, LANES), lambda s: (0, 0)),
+        ],
+        out_specs=(
+            pl.BlockSpec((members, rows, PAIR * LANES), lambda s: (0, 0, s)),
+            pl.BlockSpec((PAIR, rows, degrees), lambda s: (s, 0, 0)),
+        ),
+        scratch_shapes=[
+            pltpu.VMEM((blocks, ROWS, ROWS), jnp.bfloat16),
+            pltpu.VMEM((blocks, ROWS, ROWS), jnp.bfloat16),
+            pltpu.VMEM((blocks, ROWS, LANES), jnp.float32),
+            pltpu.VMEM((members, degrees, PAIR * LANES), jnp.bfloat16),
+        ],
+        compiler_params=pltpu.CompilerParams(vmem_limit_bytes=VMEM_LIMIT),
+        name="gradient",
+    )(grid, spec, weights, observed, bands, mixing)
+
+
+def grams_of(sums):
+    among = sums[:MEMBERS].reshape(MEMBERS, MEMBERS, NBANDS)
+    with_obs = sums[MEMBERS].reshape(1, MEMBERS, NBANDS)
+    own_obs = sums[MEMBERS + 8, :NBANDS].reshape(1, 1, NBANDS)
+    top = jnp.concatenate([among, with_obs], axis=0)
+    column = jnp.concatenate([with_obs, own_obs], axis=1)
+    column = jnp.transpose(column, (1, 0, 2))
+    full = jnp.concatenate([top, column], axis=1)
+    return jnp.transpose(full, (2, 0, 1))[None]
+
+
+def kernel_body(fourier, analysis, target, band_ids, partners, band_cotangent):
+    samples = fourier.shape[0]
+    orders = lax.axis_size("order")
+    enses = lax.axis_size("ens")
+    cores = lax.axis_size("dp")
+    own_orders = analysis.shape[1] // enses
+    core, order, ens = my_place()
+
+    weights = lax.dynamic_slice_in_dim(analysis, ens * own_orders, own_orders, 1)
     weights = jnp.transpose(weights, (1, 0, 2))
-
-    sent = fourier.reshape(samples * own_members, own_rows, parts, own_orders * width)
-    sent = jnp.transpose(sent, (2, 0, 1, 3))
-    got = lax.all_to_all(sent, ("order", "ens"), split_axis=0, concat_axis=0, tiled=True)
-    got = got.reshape(rows_parts, ens_parts, samples, own_members, own_rows, own_orders, width)
-    grid = jnp.transpose(got, (2, 5, 0, 4, 1, 3, 6))
-    grid = grid.reshape(samples, own_orders, NLAT, members * width)
-
-    spec = jnp.einsum("bmtx,mtl->bmlx", grid, weights, preferred_element_type=jnp.float32)
-    spec = jnp.where(keep[None, :, :, None], spec, 0.0).astype(jnp.bfloat16)
-    spec = spec.reshape(samples, own_orders, L, members, width)
-
-    observed = lax.all_to_all(target, "ens", split_axis=2, concat_axis=1, tiled=True)
-    observed = observed.reshape(samples, L, own_orders, width)
-    observed = jnp.transpose(observed, (0, 2, 1, 3))
-    observed = jnp.where(keep[None, :, :, None], observed, jnp.zeros((), jnp.bfloat16))
-
-    stacked = jnp.concatenate([spec, observed[:, :, :, None]], axis=3)
-    pair_terms = jnp.einsum(
-        "bmliq,bmljq->blij", stacked, stacked, preferred_element_type=jnp.float32
-    )
-    bands = lax.all_gather(band_ids[:, 0], "ens", axis=0, tiled=True)
-    band_range = jnp.arange(NBANDS, dtype=jnp.int32)
-    one_hot = (bands[:, None] == band_range[None, :]).astype(jnp.float32)
-    grams = jnp.einsum("blij,lk->bkij", pair_terms, one_hot, precision=HIGHEST)
-    grams = lax.psum(grams, ("order", "ens"))
-    sample_start = lax.axis_index("dp") * samples
-    cotangent = lax.dynamic_slice_in_dim(band_cotangent, sample_start, samples, 0)
+    band_range = jnp.arange(LANES, dtype=jnp.int32)
+    onehot = (band_ids[:, :1] == band_range[None, :]).astype(jnp.float32)
+    grid, observed, bands = gather_rows(orders, enses, fourier[0], target[0], onehot)
+    spec, sums = spectra_call(orders, enses, grid, weights, observed, bands)
+    sums = lax.psum(sums, ("order", "ens"))
+    grams = grams_of(sums)
+    cotangent = lax.dynamic_slice_in_dim(band_cotangent, core * samples, samples, 0)
     scores, mixing = band_terms(grams, partners, cotangent)
     loss_bands = lax.psum(jnp.sum(cotangent * scores, axis=0), "dp")
-
-    spread = jnp.einsum("lk,bkij->blij", one_hot, mixing, precision=HIGHEST)
-    high = lax.reduce_precision(spread, 8, 7)
-    split = jnp.concatenate([high, spread - high], axis=2).astype(jnp.bfloat16)
-    both = jnp.einsum(
-        "blij,bmljq->bmliq", split, stacked, preferred_element_type=jnp.float32
-    )
-    grad_spec = (both[:, :, :, :members] + both[:, :, :, members:]).astype(jnp.bfloat16)
-    grad_spec = grad_spec.reshape(samples, own_orders, L, members * width)
-
-    grid_grad = jnp.einsum(
-        "bmlx,mtl->bmtx", grad_spec, weights, preferred_element_type=jnp.float32
-    ).astype(jnp.bfloat16)
-    grid_grad = grid_grad.reshape(
-        samples, own_orders, rows_parts, own_rows, ens_parts, own_members, width
-    )
-    home = jnp.transpose(grid_grad, (2, 4, 0, 5, 3, 1, 6))
-    home = home.reshape(parts, samples * own_members, own_rows, own_orders * width)
-    home = lax.all_to_all(home, ("order", "ens"), split_axis=0, concat_axis=0, tiled=True)
-    grad_fourier = jnp.transpose(home, (1, 2, 0, 3)).reshape(
-        samples, own_members, own_rows, columns
-    )
-
-    weight_grad = (
-        jnp.einsum("bmtx,bmlx->tml", grid, grad_spec, preferred_element_type=jnp.float32)
-        * WEIGHT_RATIO
-    ).astype(jnp.bfloat16)
-    halves = lax.psum_scatter(weight_grad, "dp", scatter_dimension=0, tiled=True)
-    grad_analysis = lax.all_to_all(
-        halves, "ens", split_axis=0, concat_axis=1, tiled=True
-    ).astype(jnp.float32)
-    return (grad_fourier, grad_analysis, loss_bands)
+    table = jnp.transpose(mixing[0], (1, 0, 2)).reshape(ROWS, MEMBERS + 1)
+    table = jnp.pad(table, ((0, 0), (0, LANES - MEMBERS - 1)))
+    gradient, weight_grad = gradient_call(enses, grid, spec, weights, observed, bands, table)
+    home, shares = scatter_rows(orders, enses, cores, gradient, weight_grad)
+    shares = shares.reshape((cores, enses) + shares.shape[1:]).astype(jnp.float32)
+    total = jnp.transpose(jnp.sum(shares, axis=0), (2, 0, 1, 3))
+    grad_analysis = total.reshape(total.shape[0], -1, total.shape[3])
+    return (home[None], grad_analysis, loss_bands)
 
 
 def solution(mesh):
@@ -194,9 +597,17 @@
         P(),
     )
     groups = mesh.shape["order"] * mesh.shape["ens"]
-    divides = (L % groups) == 0
+    rows = NLAT // mesh.shape["order"]
+    own_orders = L // groups
+    fits = (
+        L % (groups * PAIR) == 0
+        and rows % 8 == 0
+        and L % (BLOCK * mesh.shape["ens"]) == 0
+        and NLAT % (mesh.shape["dp"] * mesh.shape["ens"] * 8) == 0
+        and mesh.shape["dp"] == 2
+    )
     return jax.shard_map(
-        joint_body if divides else body,
+        kernel_body if fits else body,
         mesh=mesh,
         in_specs=placed,
         out_specs=(P("dp", "ens", "order", None), P(("dp", "ens"), "order", None), P()),

time: 1950 us -> 1780 us (0.913); the launches traced: 1920 us -> 1780 us
  Pallas kernels: 0 us -> 1670 us
  waiting for transfers between devices: 1050 us -> 0 us
  local copies, waits for them, and re-layouts: 428 us -> 33.7 us
  matrix products: 158 us -> 0 us
  blocking collectives: 167 us -> 60.8 us
  other arithmetic: 79.3 us -> 6.44 us
  starting transfers between devices: 23.6 us -> 0 us
    pallas_call x0 -> x4, Pallas kernels: none -> 1670 us  [the longest x1 750 us: scatter_rows(): pl.pallas_call(functools.partial(scatter_kernel, orders, enses), out_shap...]
    all_to_all x4 -> x0, waiting for transfers between devices: 1020 us -> none  [the longest x1 574 us: joint_body(): lax.all_to_all(home, ('order', 'ens'), split_axis=0, concat_axis=0, tiled...]
    reshape x6 -> x1, local copies, waits for them, and re-layouts: 169 us -> 0.09 us  [grams_of(): among = sums[:MEMBERS].reshape(MEMBERS, MEMBERS, NBANDS)]
    dot_general x7 -> x0, matrix products: 158 us -> none  [the longest x1 45.4 us: joint_body(): jnp.einsum('blij,bmljq->bmliq', split, stacked, preferred_element_type=jn...]
    unnamed x1 -> x0, blocking collectives: 84.3 us -> none
    another operation x3 -> x2, local copies, waits for them, and re-layouts: 82.5 us -> 0.08 us  [the longest x1 0.08 us: grams_of(): with_obs = sums[MEMBERS].reshape(1, MEMBERS, NBANDS)]
    unnamed x28 -> x5, local copies, waits for them, and re-layouts: 91.2 us -> 24.9 us
    convert_element_type x2 -> x1, other arithmetic: 42.3 us -> 0.72 us  [kernel_body(): onehot = (band_ids[:, :1] == band_range[None, :]).astype(jnp.float32)]
  transfers between devices with their start and end apart: 5 -> 0, of which waited for: 3 -> 0; matrix products, arithmetic and copies ran while one was open for 11% -> 0% of each run, Pallas kernels for 0% -> 0%
where the time goes in v1:
time: 1780 us
  Pallas kernels  1670 us (94%)
  blocking collectives  60.8 us (3%)
  local copies, waits for them, and re-layouts  33.7 us (2%)
    pallas_call x1, Pallas kernels, scatter_rows(): pl.pallas_call(functools.partial(scatter_kernel, orders, enses), out_shap...  750 us
    pallas_call x1, Pallas kernels, gather_rows(): pl.pallas_call(functools.partial(gather_kernel, orders, enses), out_shape...  726 us
    pallas_call x1, Pallas kernels, gradient_call(): pl.pallas_call(functools.partial(gradient_kernel, enses, own_orders), gri...  108 us
    pallas_call x1, Pallas kernels, spectra_call(): pl.pallas_call(functools.partial(spectra_kernel, orders, enses, own_order...  89.2 us
    psum x1, blocking collectives, kernel_body(): sums = lax.psum(sums, ('order', 'ens'))  57.7 us

profile of v1, /device:TPU:14, one launch (start us, length us, event | category | flops | bytes accessed | tf_op | source)
XLA Modules:
  0.0 1775.3 jit_solution(5004640812919040424)
XLA Ops:
  0.6 0.7 multiply_bitcast_fusion
  1.3 0.7 slice.18
  2.0 0.8 convert_reduce_fusion.1
  2.8 0.1 copy.23
  2.9 0.7 fusion.onehot
  3.6 6.3 constant_dynamic-slice_fusion.1
  9.9 3.1 copy.30
  13.0 726.3 %gather_rows.1 = (bf16[16,320,2560]{2,1,0:T(8,128)(2,1)}, bf16[320,2560]{1,0:T(8,128)(2,1)}, f32[320,128]{1,0:T(8,128)}) custom-call(bf16[8,40,40960]{2,1,0:T(8,128)(2,1)} %bitcast.47, bf16[160,5120]{1,0:T(8,128)(2,1)} %bitcast.51, f32[160,128]{1,0:T(8,128)} %fusion.onehot), custom_call_target="tpu_custom_call" | custom-call | tf_op jit(solution)/shard_map/gather_rows/pallas_call | solution.py:202
  739.4 89.2 %spectra.1 = (bf16[16,320,2560]{2,1,0:T(8,128)(2,1)}, f32[32,256]{1,0:T(8,128)}) custom-call(bf16[16,320,2560]{2,1,0:T(8,128)(2,1)} %get-tuple-element.12.grid, bf16[20,320,320]{2,1,0:T(8,128)(2,1)} %bitcast.45, bf16[320,2560]{1,0:T(8,128)(2,1)} %get-tuple-element.13.observed, f32[320,128]{1,0:T(8,128)} %get-tuple-element.14.bands), custom_call_target="tpu_custom_call" | custom-call | tf_op jit(solution)/shard_map/spectra/pallas_call | solution.py:433
  828.6 57.7 %psum.14 = f32[32,256]{1,0:T(8,128)S(1)} all-reduce(f32[32,256]{1,0:T(8,128)} %get-tuple-element.16), channel_id=1, replica_groups=mesh['dp'=2,'order'=8,'ens'=2] {'order','ens'}, use_global_device_ids=true, to_apply=%region_1.2 | all-reduce | flops 8192 | bytes 65536 | tf_op jit(solution)/shard_map/psum | solution.py:575
  886.2 0.1 reshape_squeeze.6
  886.3 0.1 reshape.118
  886.5 0.7 gather_fusion
  887.2 0.1 sqrt_bitcast_fusion
  887.3 0.1 multiply_reduce_fusion
  887.5 3.2 psum.15
  890.7 0.1 multiply_add_fusion
  890.9 0.2 copy.26
  891.0 0.7 pad.4.mixing
  891.7 107.7 %gradient.1 = (bf16[16,320,2560]{2,1,0:T(8,128)(2,1)}, bf16[20,320,320]{2,1,0:T(8,128)(2,1)}) custom-call(bf16[16,320,2560]{2,1,0:T(8,128)(2,1)} %get-tuple-element.12.grid, bf16[16,320,2560]{2,1,0:T(8,128)(2,1)} %get-tuple-element.15.spec, bf16[20,320,320]{2,1,0:T(8,128)(2,1)} %bitcast.46, bf16[320,2560]{1,0:T(8,128)(2,1)} %get-tuple-element.13.observed, ...), custom_call_target="tpu_custom_call" | custom-call | tf_op jit(solution)/shard_map/gradient/pallas_call | solution.py:520
  999.4 750.4 %scatter_rows.1 = (bf16[8,40,40960]{2,1,0:T(8,128)(2,1)}, bf16[4,20,80,320]{3,2,1,0:T(8,128)(2,1)}) custom-call(bf16[16,320,2560]{2,1,0:T(8,128)(2,1)} %get-tuple-element.17.gradient, bf16[20,320,320]{2,1,0:T(8,128)(2,1)} %get-tuple-element.18.weight_grad), custom_call_target="tpu_custom_call" | custom-call | tf_op jit(solution)/shard_map/scatter_rows/pallas_call | solution.py:290
  1749.7 3.8 convert_reduce_fusion
  1753.5 3.8 copy.27
  1757.2 18.0 %copy.32 = bf16[1,8,40,40960]{3,2,1,0:T(8,128)(2,1)} copy(bf16[1,8,40,40960]{3,2,1,0:T(8,128)(2,1)} %bitcast.48) | data formatting | bytes 52428800
  (14 shorter events, 0.2 us)
Async XLA Ops:
  739.4 148.1 %copy-start = (f32[2,16]{1,0:T(2,128)S(1)}, f32[2,16]{1,0:T(2,128)}, u32[]{:S(2)}) copy-start(f32[2,16]{1,0:T(2,128)} %param.11) | copy-start | bytes 388
